TPU v7x, 32 devices: a whole 2x2x4 slice. The times are simulated.
32 devices in a mesh: groups: 2 (over x), tensor: 16 (over z, y, core).
Axes of the slice: x: 2, y: 2, z: 4, core: 2. Of those that a mesh axis runs over, the one named last changes fastest.
Arguments:
- tokens: bfloat16 [1024, 8192], P('groups', 'tensor'), parts along dimension 0, may hold values from -6 to 6
- norm_gain: float32 [8192], P('tensor'), may hold values from 0.1 to 1.9
- w_in: bfloat16 [8192, 3, 8192], P(None, None, 'tensor'), may hold values from -0.0625 to 0.0625
- w_short: float32 [3, 3, 8192], P(None, None, 'tensor'), may hold values from -3 to 3
- filters: bfloat16 [512, 128], P('tensor'), may hold values from -0.5 to 0.5
- skip: float32 [8192], P('tensor'), may hold values from -4 to 4
- w_out: bfloat16 [8192, 8192], P('tensor'), may hold values from -0.0625 to 0.0625
Outputs:
- mixed: bfloat16 [1024, 8192], P('groups', 'tensor'), parts along dimension 0
There are 2 independent parts, one for each index of `groups`. A program takes and returns all parts, laid end to end along the dimension named above; an argument that names none is the same for every part. Nothing has to cross between parts.
All inputs are finite; a program needn't handle non-finite values.
Results may differ from a plain program's by a relative error of at most 0.0085.
Values may be sent and summed in bfloat16 or wider, within the bound.
A program may use at most 192 MiB of HBM per device.

v0:
```python
import jax
import jax.numpy as jnp
from jax import lax
from jax.sharding import PartitionSpec as P

D = 8192


def shifted(field, lag):
    pads = ((lag, 0),) + ((0, 0),) * (field.ndim - 1)
    return jnp.pad(field, pads)[: field.shape[0]]


def lag_matrix(filters, rows):
    count, taps = filters.shape
    length = taps + rows
    line = jnp.concatenate([filters, jnp.zeros((count, rows), filters.dtype)], axis=1)
    tiled = jnp.tile(line, (1, rows))[:, : rows * (length - 1)]
    return tiled.reshape(count, rows, length - 1)[:, :, :rows]


def on_device(tokens, norm_gain, w_in, w_short, filters, skip, w_out):
    wide = tokens.astype(jnp.float32)
    squares = lax.psum(jnp.sum(wide * wide, axis=1, keepdims=True), "tensor")
    factor = lax.rsqrt(squares / D + 1e-05)
    normed = (wide * factor * norm_gain[None, :]).astype(jnp.bfloat16)
    width = w_in.shape[0]
    local = w_in.shape[2]
    rows = tokens.shape[0]
    w_flat = w_in.reshape(width, 3 * local)
    chosen = w_flat
    proj = jnp.dot(
        lax.all_gather(normed, "tensor", axis=1, tiled=True),
        chosen,
        preferred_element_type=jnp.float32,
    )
    proj = proj.reshape(rows, 3, local)
    short = w_short[0][None] * proj
    for lag in range(1, w_short.shape[0]):
        short = short + w_short[lag][None] * shifted(proj, lag)
    gated = (short[:, 1] * short[:, 2]).astype(jnp.bfloat16)
    count = filters.shape[0]
    lagged = lag_matrix(filters, rows)
    grouped = gated.reshape(rows, count, local // count)
    conv = jnp.einsum("fst,sfg->tfg", lagged, grouped, preferred_element_type=jnp.float32)
    conv = conv.reshape(rows, local)
    hidden = ((conv + skip[None, :] * gated.astype(jnp.float32)) * short[:, 0]).astype(jnp.bfloat16)
    w_cols = lax.all_to_all(w_out, "tensor", split_axis=1, concat_axis=0, tiled=True)
    chosen = w_cols
    summed = jnp.dot(
        lax.all_gather(hidden, "tensor", axis=1, tiled=True),
        chosen,
        preferred_element_type=jnp.float32,
    )
    return (wide + summed).astype(jnp.bfloat16)


def solution(mesh):
    return jax.shard_map(
        on_device,
        mesh=mesh,
        in_specs=(
            P("groups", "tensor"),
            P("tensor"),
            P(None, None, "tensor"),
            P(None, None, "tensor"),
            P("tensor", None),
            P("tensor"),
            P("tensor", None),
        ),
        out_specs=P("groups", "tensor"),
        check_vma=False,
    )
```

profile of v0, /device:TPU:0, one launch (start us, length us, event | category | flops | bytes accessed | tf_op | source)
XLA Modules:
  0.0 382.3 jit_solution(3870038537014596827)
XLA Ops:
  6.5 0.0 all-gather.3.cloned.1.call-start
  6.5 1.2 fusion.10
  7.8 35.0 %psum.7 = f32[512,1]{0,1:T(1,128)S(1)} all-reduce(f32[512,1]{0,1:T(1,128)S(1)} %bitcast.46), channel_id=1, replica_groups=mesh['groups'=2,'tensor'=16] {'tensor'}, use_global_device_ids=true, to_apply=%region_1.0 | all-reduce | flops 512 | bytes 4096 | tf_op jit(solution)/shard_map/psum | solution.py:24
  42.7 2.0 fusion.12
  44.7 0.0 all-gather.3.cloned.1.call-update
  44.8 12.1 %copy.16 = bf16[512,8192]{0,1:T(8,128)(2,1)} copy(bf16[512,8192]{1,0:T(8,128)(2,1)} %param.13) | data formatting | bytes 16777216 | tf_op args[6]
  56.8 4.8 %all-to-all-start = ((bf16[512,16,512]{0,2,1:T(8,128)(2,1)}), bf16[512,16,512]{0,2,1:T(8,128)(2,1)}, u32[]{:S(2)}, u32[]{:S(2)}) async-start(bf16[512,16,512]{0,2,1:T(8,128)(2,1)} %bitcast.41), calls=%async_computation | async-start | bytes 16777216 | tf_op jit(solution)/shard_map/all_to_all | solution.py:48
  61.6 0.0 copy-start.2
  61.6 0.0 all-gather.5.cloned.1.call-start
  61.7 33.5 %copy.13 = bf16[8192,3,512]{0,2,1:T(8,128)(2,1)} copy(bf16[8192,3,512]{2,0,1:T(8,128)(2,1)} %param.9) | data formatting | bytes 50331648 | tf_op args[2]
  95.1 0.0 copy-done.2
  95.1 2.9 tile.4
  98.0 67.1 %copy.18 = bf16[4,8,512,640]{3,1,2,0:T(8,128)(2,1)S(1)} copy(bf16[4,8,512,640]{3,2,1,0:T(8,128)(2,1)S(1)} %bitcast.39) | data formatting | bytes 41943040
  165.1 8.1 %slice.42 = bf16[32,327168]{1,0:T(8,128)(2,1)} slice(bf16[32,327680]{1,0:T(8,128)(2,1)S(1)} %bitcast.40), slice={[0:32], [0:327168]} | slice | bytes 41877504 | tf_op jit(solution)/shard_map/slice | solution.py:18
  173.2 0.0 copy-start.1
  173.2 69.0 %reshape.30 = bf16[32,512,639]{2,1,0:T(8,128)(2,1)} reshape(bf16[32,327168]{1,0:T(8,128)(2,1)} %slice.42) | data formatting | bytes 41877504 | tf_op jit(solution)/shard_map/reshape | solution.py:19
  242.2 0.0 copy-done.1
  242.3 0.0 all-gather.3.cloned.1.call-done
  242.3 19.6 %fusion = f32[512,3,512]{2,0,1:T(8,128)S(1)} fusion(bf16[8192,3,512]{0,2,1:T(8,128)(2,1)} %copy.13, bf16[512,8192]{1,0:T(8,128)(2,1)} %all-gather.3.cloned.1.call-done), kind=kOutput, calls=%fused_computation | convolution fusion | flops 12884901888 | bytes 36700160 | tf_op jit(solution)/shard_map/dot_general | solution.py:32
  261.9 0.9 fusion.7
  262.8 0.9 fusion.15
  263.8 2.1 copy.14
  265.9 0.0 copy-start.3
  265.9 9.2 %fusion.2 = f32[32,16,512]{2,1,0:T(8,128)} fusion(bf16[512,32,16]{0,2,1:T(8,128)(2,1)} %bitcast.44, bf16[32,512,639]{2,1,0:T(8,128)(2,1)} %reshape.30), kind=kOutput, calls=%fused_computation.2 | convolution fusion | flops 268435456 | bytes 18350080 | tf_op jit(solution)/shard_map/fst,sfg->tfg/dot_general | solution.py:45
  275.1 2.6 copy.15
  277.6 0.0 copy-done.3
  277.7 2.5 fusion.14
  280.2 0.0 all-gather.5.cloned.1.call-update
  280.2 0.0 all-to-all-done
  280.2 0.0 copy-start
  280.2 12.4 %copy.17 = bf16[16,512,512]{2,1,0:T(8,128)(2,1)} copy(bf16[16,512,512]{1,2,0:T(8,128)(2,1)} %bitcast.15) | data formatting | bytes 16777216 | tf_op jit(solution)/shard_map/all_to_all | solution.py:48
  292.6 71.8 %all-gather.5.cloned.1.call-done = bf16[512,8192]{1,0:T(8,128)(2,1)} async-done(((bf16[512,512]{1,0:T(8,128)(2,1)}), bf16[512,8192]{1,0:T(8,128)(2,1)}) %all-gather.5.cloned.1.call-update) | async-done | bytes 8388624 | tf_op jit(solution)/shard_map/all_gather | solution.py:51
  364.4 0.0 copy-done
  364.4 11.0 %fusion.9 = bf16[512,512]{1,0:T(8,128)(2,1)} fusion(bf16[512,8192]{1,0:T(8,128)(2,1)} %all-gather.5.cloned.1.call-done, bf16[8192,512]{1,0:T(8,128)(2,1)} %bitcast.43, bf16[512,512]{1,0:T(8,128)(2,1)S(1)} %copy-done), kind=kOutput, calls=%fused_computation.14 | convolution fusion | flops 4295753728 | bytes 17825792 | tf_op jit(solution)/shard_map/dot_general | solution.py:50
  (3 shorter events, 0.0 us)
Async XLA Ops:
  6.5 235.7 %all-gather.3.cloned.1.call-start = ((), (), s32[]{:S(2)}) async-start(), calls=%async_computation.1 | async-start | bytes 8912896 | tf_op jit(solution)/shard_map/all_gather | solution.py:33
  56.8 223.4 %all-to-all-start = ((bf16[512,16,512]{0,2,1:T(8,128)(2,1)}), bf16[512,16,512]{0,2,1:T(8,128)(2,1)}, u32[]{:S(2)}, u32[]{:S(2)}) async-start(bf16[512,16,512]{0,2,1:T(8,128)(2,1)} %bitcast.41), calls=%async_computation | async-start | bytes 16777216 | tf_op jit(solution)/shard_map/all_to_all | solution.py:48
  61.6 33.5 %copy-start.2 = (bf16[32,128]{1,0:T(8,128)(2,1)S(1)}, bf16[32,128]{1,0:T(8,128)(2,1)}, u32[]{:S(2)}) copy-start(bf16[32,128]{1,0:T(8,128)(2,1)} %param.11) | copy-start | bytes 24580
  61.6 302.8 %all-gather.5.cloned.1.call-start = ((), (), s32[]{:S(2)}) async-start(), calls=%async_computation.2 | async-start | bytes 8912896 | tf_op jit(solution)/shard_map/all_gather | solution.py:51
  173.2 69.0 %copy-start.1 = (f32[3,3,512]{2,1,0:T(4,128)S(1)}, f32[3,3,512]{2,1,0:T(4,128)}, u32[]{:S(2)}) copy-start(f32[3,3,512]{2,1,0:T(4,128)} %param.10) | copy-start | bytes 55300
  265.9 11.8 %copy-start.3 = (f32[512]{0:T(512)S(1)}, f32[512]{0:T(512)}, u32[]{:S(2)}) copy-start(f32[512]{0:T(512)} %param.12) | copy-start | bytes 6148
  280.2 84.2 %copy-start = (bf16[512,512]{1,0:T(8,128)(2,1)S(1)}, bf16[512,512]{1,0:T(8,128)(2,1)}, u32[]{:S(2)}) copy-start(bf16[512,512]{1,0:T(8,128)(2,1)} %param.7) | copy-start | bytes 1572868
Sparse Core Ops, SparseCore 0:
  44.9 189.7 all-gather.2
  280.3 84.0 all-gather.4
where the time goes:
time: 384 us; the launch traced here: 382 us
  local copies, waits for them, and re-layouts  210 us (55%)
  waiting for transfers between devices  71.8 us (19%)
  matrix products  39.9 us (10%)
  blocking collectives  35 us (9%)
  between operations  13.5 us (4%)
  other arithmetic  7.65 us (2%)
  starting transfers between devices  4.8 us (1%)
    unnamed x11, local copies, waits for them, and re-layouts  113 us
    all_gather x1, waiting for transfers between devices, on_device(): lax.all_gather(hidden, 'tensor', axis=1, tiled=True)  71.8 us
    reshape x1, local copies, waits for them, and re-layouts, lag_matrix(): return tiled.reshape(count, rows, length - 1)[:, :, :rows]  69 us
    psum x1, blocking collectives, on_device(): squares = lax.psum(jnp.sum(wide * wide, axis=1, keepdims=True), 'tensor')  35 us
    dot_general x1, matrix products, on_device(): jnp.dot(lax.all_gather(normed, 'tensor', axis=1, tiled=True), chosen, pre...  19.6 us
    all_to_all x1, local copies, waits for them, and re-layouts, on_device(): lax.all_to_all(w_out, 'tensor', split_axis=1, concat_axis=0, tiled=True)  12.4 us
    dot_general x1, matrix products, on_device(): jnp.dot(lax.all_gather(hidden, 'tensor', axis=1, tiled=True), chosen, pre...  11 us
    dot_general x1, matrix products, on_device(): jnp.einsum('fst,sfg->tfg', lagged, grouped, preferred_element_type=jnp.fl...  9.22 us
  transfers between devices with their start and end apart: 3, of which 1 were waited for; matrix products, arithmetic and copies ran while one was open for 64% of the time, Pallas kernels for 0%

commit v1 on v0

--- a/solution.py
+++ b/solution.py
@@ -21,7 +21,7 @@
 
 def on_device(tokens, norm_gain, w_in, w_short, filters, skip, w_out):
     wide = tokens.astype(jnp.float32)
-    squares = lax.psum(jnp.sum(wide * wide, axis=1, keepdims=True), "tensor")
+    squares = jnp.sum(lax.all_gather(jnp.sum(wide * wide, axis=1, keepdims=True), "tensor"), axis=0)
     factor = lax.rsqrt(squares / D + 1e-05)
     normed = (wide * factor * norm_gain[None, :]).astype(jnp.bfloat16)
     width = w_in.shape[0]

time: 384 us -> 372 us (0.969)
  blocking collectives: 35 us -> 23.2 us
    psum x1 -> x0, blocking collectives: 35 us -> none  [on_device(): squares = lax.psum(jnp.sum(wide * wide, axis=1, keepdims=True), 'tensor')]
    all_gather x0 -> x1, blocking collectives: none -> 23.2 us  [on_device(): lax.all_gather(jnp.sum(wide * wide, axis=1, keepdims=True), 'tensor')]
  transfers between devices with their start and end apart: 3 -> 3, of which waited for: 1 -> 1; matrix products, arithmetic and copies ran while one was open for 64% -> 66% of each run, Pallas kernels for 0% -> 0%
where the time goes in v1:
time: 372 us; the launch traced here: 371 us
  local copies, waits for them, and re-layouts  210 us (56%)
  waiting for transfers between devices  71.8 us (19%)
  matrix products  39.9 us (11%)
  blocking collectives  23.2 us (6%)
  between operations  13.5 us (4%)
  other arithmetic  7.69 us (2%)
  starting transfers between devices  4.8 us (1%)
    unnamed x11, local copies, waits for them, and re-layouts  113 us
    all_gather x1, waiting for transfers between devices, on_device(): lax.all_gather(hidden, 'tensor', axis=1, tiled=True)  71.8 us
    reshape x1, local copies, waits for them, and re-layouts, lag_matrix(): return tiled.reshape(count, rows, length - 1)[:, :, :rows]  69 us
    all_gather x1, blocking collectives, on_device(): lax.all_gather(jnp.sum(wide * wide, axis=1, keepdims=True), 'tensor')  23.2 us
    dot_general x1, matrix products, on_device(): jnp.dot(lax.all_gather(normed, 'tensor', axis=1, tiled=True), chosen, pre...  19.6 us
    all_to_all x1, local copies, waits for them, and re-layouts, on_device(): lax.all_to_all(w_out, 'tensor', split_axis=1, concat_axis=0, tiled=True)  12.4 us
    dot_general x1, matrix products, on_device(): jnp.dot(lax.all_gather(hidden, 'tensor', axis=1, tiled=True), chosen, pre...  11 us
    dot_general x1, matrix products, on_device(): jnp.einsum('fst,sfg->tfg', lagged, grouped, preferred_element_type=jnp.fl...  9.22 us
  transfers between devices with their start and end apart: 3, of which 1 were waited for; matrix products, arithmetic and copies ran while one was open for 66% of the time, Pallas kernels for 0%

profile of v1, /device:TPU:0, one launch (start us, length us, event | category | flops | bytes accessed | tf_op | source)
XLA Modules:
  0.0 370.6 jit_solution(11407496775047296741)
XLA Ops:
  6.5 0.0 all-gather.5.cloned.1.call-start
  6.5 1.2 fusion.10
  7.8 23.2 %all-gather.1 = f32[16,1,512]{2,1,0:T(1,128)S(1)} all-gather(f32[1,1,512]{2,1,0:T(1,128)S(1)} %bitcast.44), channel_id=2, replica_groups=mesh['groups'=2,'tensor'=16] {'tensor'}, dimensions={0}, use_global_device_ids=true | all-gather | bytes 34816 | tf_op jit(solution)/shard_map/all_gather | solution.py:24
  31.0 2.0 fusion.12
  33.0 0.0 all-gather.5.cloned.1.call-update
  33.1 12.1 %copy.21 = bf16[512,8192]{0,1:T(8,128)(2,1)} copy(bf16[512,8192]{1,0:T(8,128)(2,1)} %param.13) | data formatting | bytes 16777216 | tf_op args[6]
  45.1 4.8 %all-to-all-start = ((bf16[512,16,512]{0,2,1:T(8,128)(2,1)}), bf16[512,16,512]{0,2,1:T(8,128)(2,1)}, u32[]{:S(2)}, u32[]{:S(2)}) async-start(bf16[512,16,512]{0,2,1:T(8,128)(2,1)} %bitcast.40), calls=%async_computation | async-start | bytes 16777216 | tf_op jit(solution)/shard_map/all_to_all | solution.py:48
  49.9 0.0 copy-start.2
  49.9 0.0 all-gather.7.cloned.1.call-start
  49.9 33.5 %copy.18 = bf16[8192,3,512]{0,2,1:T(8,128)(2,1)} copy(bf16[8192,3,512]{2,0,1:T(8,128)(2,1)} %param.9) | data formatting | bytes 50331648 | tf_op args[2]
  83.4 0.0 copy-done.2
  83.4 2.9 tile.4
  86.3 67.1 %copy.23 = bf16[4,8,512,640]{3,1,2,0:T(8,128)(2,1)S(1)} copy(bf16[4,8,512,640]{3,2,1,0:T(8,128)(2,1)S(1)} %bitcast.38) | data formatting | bytes 41943040
  153.4 8.1 %slice.42 = bf16[32,327168]{1,0:T(8,128)(2,1)} slice(bf16[32,327680]{1,0:T(8,128)(2,1)S(1)} %bitcast.39), slice={[0:32], [0:327168]} | slice | bytes 41877504 | tf_op jit(solution)/shard_map/slice | solution.py:18
  161.5 0.0 copy-start.1
  161.5 69.0 %reshape.39 = bf16[32,512,639]{2,1,0:T(8,128)(2,1)} reshape(bf16[32,327168]{1,0:T(8,128)(2,1)} %slice.42) | data formatting | bytes 41877504 | tf_op jit(solution)/shard_map/reshape | solution.py:19
  230.5 0.0 copy-done.1
  230.5 0.0 all-gather.5.cloned.1.call-done
  230.6 19.6 %fusion = f32[512,3,512]{2,0,1:T(8,128)S(1)} fusion(bf16[8192,3,512]{0,2,1:T(8,128)(2,1)} %copy.18, bf16[512,8192]{1,0:T(8,128)(2,1)} %all-gather.5.cloned.1.call-done), kind=kOutput, calls=%fused_computation | convolution fusion | flops 12884901888 | bytes 36700160 | tf_op jit(solution)/shard_map/dot_general | solution.py:32
  250.2 0.9 fusion.7
  251.1 0.9 fusion.15
  252.1 2.1 copy.19
  254.1 0.0 copy-start.3
  254.1 9.2 %fusion.2 = f32[32,16,512]{2,1,0:T(8,128)} fusion(bf16[512,32,16]{0,2,1:T(8,128)(2,1)} %bitcast.43, bf16[32,512,639]{2,1,0:T(8,128)(2,1)} %reshape.39), kind=kOutput, calls=%fused_computation.2 | convolution fusion | flops 268435456 | bytes 18350080 | tf_op jit(solution)/shard_map/fst,sfg->tfg/dot_general | solution.py:45
  263.4 2.6 copy.20
  265.9 0.0 copy-done.3
  265.9 2.5 fusion.14
  268.5 0.0 all-gather.7.cloned.1.call-update
  268.5 0.0 all-to-all-done
  268.5 0.0 copy-start
  268.5 12.4 %copy.22 = bf16[16,512,512]{2,1,0:T(8,128)(2,1)} copy(bf16[16,512,512]{1,2,0:T(8,128)(2,1)} %bitcast.14) | data formatting | bytes 16777216 | tf_op jit(solution)/shard_map/all_to_all | solution.py:48
  280.9 71.8 %all-gather.7.cloned.1.call-done = bf16[512,8192]{1,0:T(8,128)(2,1)} async-done(((bf16[512,512]{1,0:T(8,128)(2,1)}), bf16[512,8192]{1,0:T(8,128)(2,1)}) %all-gather.7.cloned.1.call-update) | async-done | bytes 8388624 | tf_op jit(solution)/shard_map/all_gather | solution.py:51
  352.7 0.0 copy-done
  352.7 11.0 %fusion.9 = bf16[512,512]{1,0:T(8,128)(2,1)} fusion(bf16[512,8192]{1,0:T(8,128)(2,1)} %all-gather.7.cloned.1.call-done, bf16[8192,512]{1,0:T(8,128)(2,1)} %bitcast.42, bf16[512,512]{1,0:T(8,128)(2,1)S(1)} %copy-done), kind=kOutput, calls=%fused_computation.14 | convolution fusion | flops 4295753728 | bytes 17825792 | tf_op jit(solution)/shard_map/dot_general | solution.py:50
  (4 shorter events, 0.1 us)
Async XLA Ops:
  6.5 224.0 %all-gather.5.cloned.1.call-start = ((), (), s32[]{:S(2)}) async-start(), calls=%async_computation.1 | async-start | bytes 8912896 | tf_op jit(solution)/shard_map/all_gather | solution.py:33
  45.1 223.4 %all-to-all-start = ((bf16[512,16,512]{0,2,1:T(8,128)(2,1)}), bf16[512,16,512]{0,2,1:T(8,128)(2,1)}, u32[]{:S(2)}, u32[]{:S(2)}) async-start(bf16[512,16,512]{0,2,1:T(8,128)(2,1)} %bitcast.40), calls=%async_computation | async-start | bytes 16777216 | tf_op jit(solution)/shard_map/all_to_all | solution.py:48
  49.9 33.5 %copy-start.2 = (bf16[32,128]{1,0:T(8,128)(2,1)S(1)}, bf16[32,128]{1,0:T(8,128)(2,1)}, u32[]{:S(2)}) copy-start(bf16[32,128]{1,0:T(8,128)(2,1)} %param.11) | copy-start | bytes 24580
  49.9 302.8 %all-gather.7.cloned.1.call-start = ((), (), s32[]{:S(2)}) async-start(), calls=%async_computation.2 | async-start | bytes 8912896 | tf_op jit(solution)/shard_map/all_gather | solution.py:51
  161.5 69.0 %copy-start.1 = (f32[3,3,512]{2,1,0:T(4,128)S(1)}, f32[3,3,512]{2,1,0:T(4,128)}, u32[]{:S(2)}) copy-start(f32[3,3,512]{2,1,0:T(4,128)} %param.10) | copy-start | bytes 55300
  254.1 11.8 %copy-start.3 = (f32[512]{0:T(512)S(1)}, f32[512]{0:T(512)}, u32[]{:S(2)}) copy-start(f32[512]{0:T(512)} %param.12) | copy-start | bytes 6148
  268.5 84.2 %copy-start = (bf16[512,512]{1,0:T(8,128)(2,1)S(1)}, bf16[512,512]{1,0:T(8,128)(2,1)}, u32[]{:S(2)}) copy-start(bf16[512,512]{1,0:T(8,128)(2,1)} %param.7) | copy-start | bytes 1572868
Sparse Core Ops, SparseCore 0:
  33.2 189.7 all-gather.4
  268.6 84.0 all-gather.6
